TPU v7x, 512 devices: a whole 4x8x8 slice. The times are simulated.
512 devices in a mesh: star: 16 (over y, core), cad: 32 (over z, x).
Axes of the slice: x: 4, y: 8, z: 8, core: 2. Of those that a mesh axis runs over, the one named last changes fastest.
Arguments:
- light: float32 [65536, 8192], P('star', 'cad'), may hold values from -2000 to 2000
- quality: int32 [8192], P('cad'), may hold values 0 or 1
- star_factors: float32 [65536, 128], P('star', 'cad'), may hold values from -6 to 6
- cadence_factors: float32 [8192, 128], P('cad', 'star'), may hold values from -6 to 6
Outputs:
- star_gradient: float32 [65536, 128], P('star', 'cad')
- cadence_gradient: float32 [8192, 128], P('cad', 'star')
- loss: float32 [], replicated
All inputs are finite; a program needn't handle non-finite values. No bound on the sum of `quality` on one device may be relied on, other than what follows from the above.
Results may differ from a plain program's by a relative error of at most 0.0003.
Values sent between devices are 32-bit elements; how exact they have to be, the bound alone decides.
A program may use at most 64 MiB of HBM per device.

v0:
```python
import jax
import jax.numpy as jnp
from jax import lax
from jax.sharding import PartitionSpec as P


def on_device(light, quality, star_factors, cadence_factors):
    star_count = light.shape[0] * lax.axis_size("star")
    cad_count = light.shape[1] * lax.axis_size("cad")
    star_loads = lax.all_gather(star_factors, "cad", axis=1, tiled=True)
    cad_loads = lax.all_gather(cadence_factors, "star", axis=1, tiled=True)
    predicted = jnp.dot(
        star_loads, cad_loads.T, precision=lax.Precision.HIGHEST, preferred_element_type=jnp.float32
    )
    residual = light - predicted
    ratio = 1.0 + (residual * 0.5) ** 2
    good = quality.astype(jnp.float32)[None, :]
    weighted = good * residual / ratio
    loss_part = jnp.sum(good * 2.0 * jnp.log(ratio))
    star_term = jnp.dot(
        weighted, cad_loads, precision=lax.Precision.HIGHEST, preferred_element_type=jnp.float32
    )
    cad_term = jnp.dot(
        weighted.T, star_loads, precision=lax.Precision.HIGHEST, preferred_element_type=jnp.float32
    )
    star_width = star_factors.shape[1]
    cad_width = cadence_factors.shape[1]
    star_full, loss_cad = lax.psum((star_term, loss_part), "cad")
    cad_full, loss_all = lax.psum((cad_term, loss_cad), "star")
    star_sum = lax.dynamic_slice_in_dim(
        star_full, lax.axis_index("cad") * star_width, star_width, 1
    )
    cad_sum = lax.dynamic_slice_in_dim(cad_full, lax.axis_index("star") * cad_width, cad_width, 1)
    star_gradient = -star_sum / jnp.sqrt(jnp.float32(cad_count))
    cadence_gradient = -cad_sum / jnp.sqrt(jnp.float32(star_count))
    loss = loss_all / (jnp.float32(star_count) * jnp.float32(cad_count))
    return (star_gradient, cadence_gradient, loss)


def solution(mesh):
    in_specs = (P("star", "cad"), P("cad"), P("star", "cad"), P("cad", "star"))
    out_specs = (P("star", "cad"), P("cad", "star"), P())
    return jax.shard_map(
        on_device, mesh=mesh, in_specs=in_specs, out_specs=out_specs, check_vma=False
    )
```

profile of v0, /device:TPU:8, one launch (start us, length us, event | category | flops | bytes accessed | tf_op | source)
XLA Modules:
  0.0 403.6 jit_solution(11377045682946022342)
XLA Ops:
  7.2 0.0 all-gather.3.cloned.1.call-start
  7.2 0.7 all-gather.3.cloned.1.call-update
  7.9 0.0 all-reduce.5.cloned.1.call-start
  7.9 0.7 convert_element_type.3
  8.6 20.5 %all_gather.7 = f32[256,128]{0,1:T(8,128)S(1)} all-gather(f32[256,8]{0,1:T(8,128)} %param.7), channel_id=1, replica_groups=mesh['star'=16,'cad'=32] {'star'}, dimensions={1}, use_global_device_ids=true | all-gather | bytes 139264 | tf_op jit(solution)/shard_map/all_gather | solution.py:11
  29.1 0.7 broadcast_multiply_fusion
  29.8 70.0 %all-gather.3.cloned.1.call-done = f32[32,4,4096]{2,1,0:T(4,128)} async-done(((f32[1,4,4096]{2,1,0:T(4,128)}), f32[32,4,4096]{2,1,0:T(4,128)}) %all-gather.3.cloned.1.call-update) | async-done | bytes 2097168 | tf_op jit(solution)/shard_map/all_gather | solution.py:10
  99.8 2.0 reshape.10
  101.7 6.7 %multiply_reduce_fusion = (f32[]{:T(128)}, f32[4096,256]{1,0:T(8,128)S(1)}) fusion(f32[256]{0:T(256)S(1)} %broadcast_multiply_fusion, f32[4096,256]{1,0:T(8,128)} %param.4, f32[128,4096]{1,0:T(8,128)S(1)} %reshape.10, f32[256,128]{0,1:T(8,128)S(1)} %all_gather.7), kind=kOutput, calls=%fused_computation.1 | convolution fusion | flops 1616904192 | bytes 10617860 | tf_op jit(solution)/shard_map/dot_general | solution.py:12
  108.5 0.0 copy-start
  108.5 1.9 copy-done
  110.4 4.0 fusion
  114.4 0.0 all-reduce.5.cloned.1.call-update
  114.5 0.0 all-reduce.3.cloned.1.call-start
  114.5 8.8 %fusion.1 = f32[4096,128]{0,1:T(8,128)} fusion(f32[256,128]{0,1:T(8,128)S(1)} %all_gather.7, f32[4096,256]{1,0:T(8,128)} %copy-done, f32[256]{0:T(256)S(1)} %convert_element_type.3), kind=kOutput, calls=%fused_computation.5 | convolution fusion | flops 1615855616 | bytes 6423552 | tf_op jit(solution)/shard_map/dot_general | solution.py:20
  123.3 0.0 all-reduce.3.cloned.1.call-update
  123.3 72.8 %psum.30 = f32[]{:T(128)} all-reduce(f32[]{:T(128)} %get-tuple-element.3), channel_id=1, replica_groups=mesh['star'=16,'cad'=32] {'cad'}, use_global_device_ids=true, to_apply=%region_3.0 | all-reduce | flops 1 | bytes 8 | tf_op jit(solution)/shard_map/psum | solution.py:28
  196.1 21.2 %psum.31 = f32[]{:T(128)} all-reduce(f32[]{:T(128)} %psum.30), channel_id=1, replica_groups=mesh['star'=16,'cad'=32] {'star'}, use_global_device_ids=true, to_apply=%region_4.0 | all-reduce | flops 1 | bytes 8 | tf_op jit(solution)/shard_map/psum | solution.py:29
  217.9 4.7 %all-reduce.5.cloned.1.call-done = f32[256,128]{0,1:T(8,128)} async-done(((f32[256,128]{0,1:T(8,128)}), f32[256,128]{0,1:T(8,128)}) %all-reduce.5.cloned.1.call-update) | async-done | bytes 131088 | tf_op jit(solution)/shard_map/psum | solution.py:29
  222.6 1.3 negate_multiply_fusion.1
  223.9 170.5 %all-reduce.3.cloned.1.call-done = f32[4096,128]{0,1:T(8,128)} async-done(((f32[4096,128]{0,1:T(8,128)}), f32[4096,128]{0,1:T(8,128)}) %all-reduce.3.cloned.1.call-update) | async-done | bytes 2097168 | tf_op jit(solution)/shard_map/psum | solution.py:28
  394.4 1.6 negate_multiply_fusion
Async XLA Ops:
  7.2 92.6 %all-gather.3.cloned.1.call-start = ((), (), s32[]{:S(2)}) async-start(), calls=%async_computation.2 | async-start | bytes 2162688 | tf_op jit(solution)/shard_map/all_gather | solution.py:10
  7.9 214.7 %all-reduce.5.cloned.1.call-start = ((), (), s32[]{:S(2)}) async-start(), calls=%async_computation.1 | async-start | bytes 262144 | tf_op jit(solution)/shard_map/psum | solution.py:29
  108.5 1.9 copy-start
  114.5 279.9 %all-reduce.3.cloned.1.call-start = ((), (), s32[]{:S(2)}) async-start(), calls=%async_computation | async-start | bytes 4194304 | tf_op jit(solution)/shard_map/psum | solution.py:28
Sparse Core Ops, SparseCore 0:
  11.2 88.5 all-gather.2
  114.6 107.9 all-reduce.4
  226.5 167.8 all-reduce.2
where the time goes:
time: 404 us
  waiting for transfers between devices  246 us (61%)
  blocking collectives  114 us (28%)
  matrix products  19.5 us (5%)
  between operations  15.5 us (4%)
  other arithmetic  4.21 us (1%)
    psum x1, waiting for transfers between devices, on_device(): star_full, loss_cad = lax.psum((star_term, loss_part), 'cad')  170 us
    psum x1, blocking collectives, on_device(): star_full, loss_cad = lax.psum((star_term, loss_part), 'cad')  72.8 us
    all_gather x1, waiting for transfers between devices, on_device(): star_loads = lax.all_gather(star_factors, 'cad', axis=1, tiled=True)  70 us
    psum x1, blocking collectives, on_device(): cad_full, loss_all = lax.psum((cad_term, loss_cad), 'star')  21.2 us
    all_gather x1, blocking collectives, on_device(): cad_loads = lax.all_gather(cadence_factors, 'star', axis=1, tiled=True)  20.5 us
    dot_general x1, matrix products, on_device(): jnp.dot(weighted, cad_loads, precision=lax.Precision.HIGHEST, preferred_e...  8.77 us
  transfers between devices with their start and end apart: 3, of which 3 were waited for; matrix products, arithmetic and copies ran while one was open for 3% of the time, Pallas kernels for 0%

commit v1 on v0

v1 whole, which is shorter than its diff:
```python
import functools

import jax
import jax.numpy as jnp
from jax import lax
from jax.experimental import pallas as pl
from jax.experimental.pallas import tpu as pltpu
from jax.sharding import PartitionSpec as P

MESH = pl.DeviceIdType.MESH
F32, BF16 = jnp.float32, jnp.bfloat16
NZ, NX, NY = 8, 4, 8
HALF = 2048
CADS = 256
BLOCK = 256
CHUNKS = (("xz", 0, 512), ("zx", 512, 512), ("xz", 1024, 512), ("zx", 1536, 512))
MESSAGES = 10


def split(value):
    high = value.astype(BF16)
    return high, (value - high.astype(F32)).astype(BF16)


def dot3(a, b, dims):
    def one(p, q):
        return lax.dot_general(p, q, (dims, ((), ())), preferred_element_type=F32)

    return one(a[0], b[0]) + (one(a[0], b[1]) + one(a[1], b[0]))


def kernel(
    star_scale, cad_scale, loss_scale,
    light_ref, quality_ref, star_ref, cad_ref,
    star_out, cad_out, loss_out,
    light, own, slabs, grads, cads, expanded, wide_high, wide_low, good, acc, logs,
    cad_part, cad_core, cad_from, loss_x, loss_z, *rest,
):
    boxes, (sems, gather_send, gather_recv, reduce_send, reduce_recv, small_send, small_recv) = rest[:-7], rest[-7:]
    star, cad = lax.axis_index("star"), lax.axis_index("cad")
    y, core = star // 2, lax.rem(star, 2)
    z, x = cad // NX, lax.rem(cad, NX)

    def at_z(d):
        return lax.rem(z + d + NZ, NZ)

    def at_x(d):
        return lax.rem(x + d + NX, NX)

    def at_y(d):
        return lax.rem(y + d, NY)

    def to_z(d):
        return (star, at_z(d) * NX + x)

    def to_x(d):
        return (star, z * NX + at_x(d))

    def to_y(d):
        return (at_y(d) * 2 + core, cad)

    partner = (y * 2 + 1 - core, cad)

    light_copy = pltpu.make_async_copy(light_ref, light, sems.at[0])
    own_copy = pltpu.make_async_copy(star_ref, own, sems.at[1])
    cad_copy = pltpu.make_async_copy(cad_ref, cads.at[y, core], sems.at[2])
    good_copy = pltpu.make_async_copy(quality_ref, good, sems.at[3])
    own_copy.start()
    cad_copy.start()
    good_copy.start()

    barrier = pltpu.get_barrier_semaphore()
    peers = [to_z(d) for d in range(1, NZ)] + [to_x(d) for d in range(1, NX)]
    peers += [to_y(d) for d in range(1, NY)] + [partner]
    for peer in peers:
        pl.semaphore_signal(barrier, inc=1, device_id=peer, device_id_type=MESH)
    own_copy.wait()
    slabs[z, x, 0:4, :] = own[:, :HALF]
    slabs[z, x, 4:8, :] = own[:, HALF:]
    pl.semaphore_wait(barrier, len(peers))

    def remote(src, dst, send, recv, where):
        copy = pltpu.make_async_remote_copy(
            src_ref=src, dst_ref=dst, send_sem=send, recv_sem=recv,
            device_id=where, device_id_type=MESH,
        )
        copy.start()
        return copy

    sent = []

    def gather_rounds(index, order, first, width):
        columns = pl.ds(first, width)
        count = [0]

        def view(ref, axis, place):
            if axis == order[0]:
                return ref.at[(place, x) if axis == "z" else (z, place)].at[:, columns]
            if axis == "z":
                return ref.at[place].at[:, :, columns]
            return ref.at[:, place].at[:, :, columns]

        def send(axis, origin, step):
            block = view(slabs, axis, origin)
            n = index * MESSAGES + count[0]
            count[0] += 1
            where = to_z(step) if axis == "z" else to_x(step)
            copy = remote(block, block, gather_send.at[n], gather_recv.at[n], where)
            sent.append(copy)
            return copy

        up = {}
        odd = index // 2 % 2
        for axis in order:
            at, size = (at_z, NZ) if axis == "z" else (at_x, NX)
            right, left = send(axis, at(0), 1), send(axis, at(0), -1)
            yield
            for hop in range(1, size // 2):
                last = hop == size // 2 - 1
                right.wait_recv()
                if not last or not odd:
                    right_next = send(axis, at(-hop), 1)
                left.wait_recv()
                if not last or odd:
                    left = send(axis, at(hop), -1)
                if not last or not odd:
                    right = right_next
                yield
            (left if odd else right).wait_recv()

    def reduce_rounds(index, order, first, width, box_far, box_near):
        columns = pl.ds(first, width)
        count = [0]

        def view(axis, place):
            if axis == order[0]:
                return grads.at[(place, x) if axis == "z" else (z, place)].at[:, columns]
            if axis == "z":
                return grads.at[place].at[:, :, columns]
            return grads.at[:, place].at[:, :, columns]

        odd = index // 2 % 2
        for axis, box in ((order[1], box_far), (order[0], box_near)):
            at, size = (at_z, NZ) if axis == "z" else (at_x, NX)
            far = size // 2
            slot = [0]

            def send(owner, step):
                n = index * MESSAGES + count[0]
                count[0] += 1
                where = to_z(step) if axis == "z" else to_x(step)
                landing = box.at[slot[0]]
                slot[0] += 1
                copy = remote(view(axis, owner), landing, reduce_send.at[n], reduce_recv.at[n], where)
                sent.append(copy)
                return copy, landing

            def take(arrived, owner):
                arrived[0].wait_recv()
                mine = view(axis, owner)
                mine[...] = mine[...] + arrived[1][...]

            sign = 1 if odd else -1
            long = send(at(sign * far), sign)
            short = send(at(-sign * (far - 1)), -sign)
            yield
            for hop in range(1, far):
                take(long, at(sign * (far - hop)))
                long = send(at(sign * (far - hop)), sign)
                if hop < far - 1:
                    take(short, at(-sign * (far - 1 - hop)))
                    short = send(at(-sign * (far - 1 - hop)), -sign)
                yield
            take(short, at(0))
            take(long, at(0))

    cad_copy.wait()
    cad_in = [
        remote(cads.at[y, core], cads.at[y, core], small_send.at[d - 1], small_recv.at[d - 1], to_y(d))
        for d in range(1, NY)
    ]
    sent.extend(cad_in)
    gathers = [gather_rounds(i, *chunk) for i, chunk in enumerate(CHUNKS)]
    for g in gathers:
        next(g)
    light_copy.start()
    for g in gathers:
        next(g)
    for copy in cad_in:
        copy.wait_recv()
    cad_across = remote(cads.at[:, core], cads.at[:, core], small_send.at[7], small_recv.at[7], partner)
    sent.append(cad_across)
    for g in gathers:
        next(g)
    cad_across.wait_recv()

    good_copy.wait()
    keep = good[...].astype(F32)
    values = cads[...].reshape(16, 8, CADS) * keep[None]
    turned = pltpu.roll(values, 4, 1)
    upper = lax.broadcasted_iota(jnp.int32, (16, 8, CADS), 1) < 4
    zero = jnp.zeros_like(values)
    expanded[:, 0, :, :CADS] = jnp.where(upper, values, zero)
    expanded[:, 1, :, :CADS] = jnp.where(upper, turned, zero)
    expanded[:, 0, :, CADS:] = jnp.where(upper, zero, turned)
    expanded[:, 1, :, CADS:] = jnp.where(upper, zero, values)
    high, low = split(expanded[...].reshape(256, 2 * CADS))
    wide_high[...] = high
    wide_low[...] = low
    acc[...] = jnp.zeros_like(acc)
    logs[...] = jnp.zeros_like(logs)

    going = True
    while going:
        going = False
        for g in gathers:
            try:
                next(g)
                going = True
            except StopIteration:
                pass
    light_copy.wait()

    def block(j, carry):
        columns = pl.ds(pl.multiple_of(j * BLOCK, BLOCK), BLOCK)
        loads = slabs[:, :, :, columns].reshape(256, BLOCK)
        wide = (wide_high[...], wide_low[...])
        predicted = dot3(split(loads.T), wide, ((1,), (0,)))
        keep = good[...].astype(F32)
        weighted = []
        for half in range(2):
            rows = pl.ds(pl.multiple_of(half * HALF + j * BLOCK, BLOCK), BLOCK)
            side = slice(half * CADS, (half + 1) * CADS)
            residual = light[rows, :] * keep - predicted[:, side]
            ratio = 1.0 + (residual * 0.5) ** 2
            weighted.append(residual / ratio)
            four = ratio.reshape(4, BLOCK // 4, CADS)
            four = (four[0] * four[1]) * (four[2] * four[3])
            logs[:, side] += jnp.sum(jnp.log(four).reshape(BLOCK // 32, 8, CADS), axis=0)
        weighted = split(jnp.concatenate(weighted, axis=1))
        grads[:, :, :, columns] = dot3(wide, weighted, ((1,), (1,))).reshape(NZ, NX, 8, BLOCK)
        acc[...] += dot3(split(loads), weighted, ((1,), (0,))).reshape(acc.shape)
        return carry

    lax.fori_loop(0, HALF // BLOCK, block, 0)

    reduces = [reduce_rounds(i, *chunk, boxes[2 * i], boxes[2 * i + 1]) for i, chunk in enumerate(CHUNKS)]
    for g in reduces:
        next(g)

    top = lax.broadcasted_iota(jnp.int32, (16, 8, CADS), 1) < 4
    first, second = acc[:, 0, :, :], acc[:, 1, :, :]
    sums = jnp.where(
        top,
        first[:, :, :CADS] + pltpu.roll(first[:, :, CADS:], 4, 1),
        pltpu.roll(second[:, :, :CADS], 4, 1) + second[:, :, CADS:],
    )
    cad_part[:, :, 0:8, :] = sums.reshape(NY, 2, 8, CADS)
    log_sum = (logs[:, :CADS] + logs[:, CADS:])
    cad_part[:, :, 8:16, :] = jnp.broadcast_to(log_sum[None, None], (NY, 2, 8, CADS))
    across = remote(cad_part.at[:, 1 - core], cad_core, small_send.at[8], small_recv.at[8], partner)
    sent.append(across)
    for g in reduces:
        next(g)
    across.wait_recv()
    cad_part[:, core] = cad_part[:, core] + cad_core[...]
    arrivals = [
        remote(cad_part.at[at_y(d), core], cad_from.at[y], small_send.at[8 + d], small_recv.at[8 + d], to_y(d))
        for d in range(1, NY)
    ]
    sent.extend(arrivals)
    for g in reduces:
        next(g)
    cad_from[y] = cad_part[y, core]
    for copy in arrivals:
        copy.wait_recv()
    total = jnp.sum(cad_from[...], axis=0)
    cad_out[...] = total[0:8] * cad_scale
    loss_x[x] = total[8:16]
    loss_hops = [
        remote(loss_x.at[x], loss_x.at[x], small_send.at[15 + d], small_recv.at[15 + d], to_x(d))
        for d in range(1, NX)
    ]
    sent.extend(loss_hops)
    for g in reduces:
        next(g)
    for copy in loss_hops:
        copy.wait_recv()
    loss_z[z] = jnp.sum(loss_x[...], axis=0)
    loss_hops = [
        remote(loss_z.at[z], loss_z.at[z], small_send.at[18 + d], small_recv.at[18 + d], to_z(d))
        for d in range(1, NZ)
    ]
    sent.extend(loss_hops)
    for g in reduces:
        next(g)
    going = True
    while going:
        going = False
        for g in reduces:
            try:
                next(g)
                going = True
            except StopIteration:
                pass
    for copy in loss_hops:
        copy.wait_recv()
    everything = jnp.sum(loss_z[...], axis=0)
    loss_out[...] = jnp.sum(jnp.sum(everything, axis=0, keepdims=True), axis=1, keepdims=True) * loss_scale
    star_out[:, :HALF] = slabs_out(grads, z, x, 0) * star_scale
    star_out[:, HALF:] = slabs_out(grads, z, x, 4) * star_scale
    for copy in sent:
        copy.wait_send()


def slabs_out(grads, z, x, row):
    return grads[z, x, row:row + 4, :]


def on_device(light, quality, star_factors, cadence_factors):
    stars = light.shape[0] * lax.axis_size("star")
    cads = light.shape[1] * lax.axis_size("cad")
    dma = pltpu.SemaphoreType.DMA
    boxes = []
    for order, _, width in CHUNKS:
        far, near = ((NX, NZ) if order == "xz" else (NZ, NX))
        hops = {NX: 3, NZ: 7}
        boxes.append(pltpu.VMEM((hops[near], far, 8, width), F32))
        boxes.append(pltpu.VMEM((hops[far], 8, width), F32))
    count = len(CHUNKS) * MESSAGES
    any_space = pl.BlockSpec(memory_space=pl.ANY)
    vmem = pl.BlockSpec(memory_space=pltpu.VMEM)
    star_gradient, cadence_gradient, loss = pl.pallas_call(
        functools.partial(
            kernel, -1.0 / float(cads) ** 0.5, -1.0 / float(stars) ** 0.5, 2.0 / (float(stars) * float(cads))
        ),
        out_shape=(
            jax.ShapeDtypeStruct((4, 4096), F32),
            jax.ShapeDtypeStruct((8, CADS), F32),
            jax.ShapeDtypeStruct((1, 1), F32),
        ),
        in_specs=[any_space] * 4,
        out_specs=(vmem, vmem, vmem),
        scratch_shapes=[
            pltpu.VMEM((4096, CADS), F32),
            pltpu.VMEM((4, 4096), F32),
            pltpu.VMEM((NZ, NX, 8, HALF), F32),
            pltpu.VMEM((NZ, NX, 8, HALF), F32),
            pltpu.VMEM((NY, 2, 8, CADS), F32),
            pltpu.VMEM((16, 2, 8, 2 * CADS), F32),
            pltpu.VMEM((256, 2 * CADS), BF16),
            pltpu.VMEM((256, 2 * CADS), BF16),
            pltpu.VMEM((1, CADS), jnp.int32),
            pltpu.VMEM((16, 2, 8, 2 * CADS), F32),
            pltpu.VMEM((8, 2 * CADS), F32),
            pltpu.VMEM((NY, 2, 16, CADS), F32),
            pltpu.VMEM((NY, 16, CADS), F32),
            pltpu.VMEM((NY, 16, CADS), F32),
            pltpu.VMEM((NX, 8, CADS), F32),
            pltpu.VMEM((NZ, 8, CADS), F32),
            *boxes,
            dma((4,)),
            dma((count,)), dma((count,)), dma((count,)), dma((count,)), dma((26,)), dma((26,)),
        ],
        compiler_params=pltpu.CompilerParams(
            collective_id=0, has_side_effects=True, vmem_limit_bytes=60 << 20
        ),
        cost_estimate=pl.CostEstimate(flops=10**9, bytes_accessed=5 * 10**6, transcendentals=2 * 10**6),
        name="cauchy_factor_gradient",
    )(light, quality.reshape(1, CADS), star_factors.T, cadence_factors.T)
    return (star_gradient.T, cadence_gradient.T, loss.reshape(()))


def solution(mesh):
    in_specs = (P("star", "cad"), P("cad"), P("star", "cad"), P("cad", "star"))
    out_specs = (P("star", "cad"), P("cad", "star"), P())
    return jax.shard_map(
        on_device, mesh=mesh, in_specs=in_specs, out_specs=out_specs, check_vma=False
    )
```

time: 404 us -> 79.6 us (0.20)
  the two profiles are of different devices: /device:TPU:8 before, /device:TPU:2 now
where the time goes in v1:
time: 79.6 us; the launch traced here: 79.4 us
  Pallas kernels  74.3 us (93%)
  local copies, waits for them, and re-layouts  2.77 us (3%)
  between operations  2.33 us (3%)
    pallas_call x1, Pallas kernels, on_device(): pl.pallas_call(functools.partial(kernel, -1.0 / float(cads) ** 0.5, -1.0...  74.3 us
    unnamed x2, local copies, waits for them, and re-layouts  2.77 us

profile of v1, /device:TPU:2, one launch (start us, length us, event | category | flops | bytes accessed | tf_op | source)
XLA Modules:
  0.0 79.4 jit_solution(8649569832449783804)
XLA Ops:
  0.6 74.3 %cauchy_factor_gradient.1 = (f32[4,4096]{1,0:T(4,128)}, f32[8,256]{1,0:T(8,128)}, f32[1,1]{1,0:T(1,128)}) custom-call(f32[4096,256]{1,0:T(8,128)} %light_ref.1, s32[1,256]{1,0:T(1,128)} %bitcast.10, f32[4,4096]{1,0:T(4,128)} %bitcast.6, f32[8,256]{1,0:T(8,128)} %bitcast.8), custom_call_target="tpu_custom_call" | custom-call | flops 1000000000 | bytes 5000000 | tf_op jit(solution)/shard_map/cauchy_factor_gradient/pallas_call | solution.py:333
  74.9 1.5 %copy.10 = f32[4096,4]{0,1:T(4,128)} copy(f32[4096,4]{0,1:T(4,128)} %bitcast.7) | data formatting | bytes 131072
  76.4 1.3 %copy.11 = f32[256,8]{0,1:T(8,128)} copy(f32[256,8]{0,1:T(8,128)} %bitcast.9) | data formatting | bytes 16384

commit v2 on v1

--- a/solution.py
+++ b/solution.py
@@ -13,8 +13,49 @@
 HALF = 2048
 CADS = 256
 BLOCK = 256
-CHUNKS = (("xz", 0, 512), ("zx", 512, 512), ("xz", 1024, 512), ("zx", 1536, 512))
-MESSAGES = 10
+EDGES = NZ * NX - 1
+STEP_Z = (
+    (0, 0, 0, 0),
+    (1, 0, 0, 0),
+    (1, 1, 1, 0),
+    (2, 0, 0, 0),
+    (1, 1, -2, 0),
+    (-1, -1, 0, 0),
+    (-1, -2, 0, 0),
+    (-1, 0, -1, 0),
+)
+STEP_X = (
+    (0, 1, -1, -1),
+    (0, 1, 1, -1),
+    (0, 0, 0, -1),
+    (0, 1, 1, -1),
+    (0, 0, 0, -1),
+    (0, 0, 1, -1),
+    (0, 0, 1, -1),
+    (0, 1, 0, -1),
+)
+
+
+def tree():
+    parents = {
+        (dz, dx): ((dz - STEP_Z[dz][dx]) % NZ, (dx - STEP_X[dz][dx]) % NX)
+        for dz in range(NZ)
+        for dx in range(NX)
+        if dz or dx
+    }
+
+    def depth(place):
+        return 1 + depth(parents[place]) if place in parents else 0
+
+    levels = [[] for _ in range(max(map(depth, parents)))]
+    for place, parent in parents.items():
+        levels[depth(place) - 1].append((place, parent))
+    return levels
+
+
+TREE = tree()
+LEVELS = len(TREE)
+CHUNKS = ((0, 256), (256, 768), (1024, 512), (1536, 512))
 
 
 def split(value):
@@ -89,90 +130,62 @@
 
     sent = []
 
-    def gather_rounds(index, order, first, width):
+    def whole(offset):
+        return (at_z(offset[0]), at_x(offset[1]))
+
+    def minus(a, b=(0, 0)):
+        return (b[0] - a[0], b[1] - a[1])
+
+    def device(offset):
+        places = whole(offset)
+        return (star, places[0] * NX + places[1])
+
+    def wait_for(ref, semaphore):
+        pltpu.make_async_copy(ref, ref, semaphore).wait()
+
+    def gather_rounds(index, first, width):
         columns = pl.ds(first, width)
-        count = [0]
-
-        def view(ref, axis, place):
-            if axis == order[0]:
-                return ref.at[(place, x) if axis == "z" else (z, place)].at[:, columns]
-            if axis == "z":
-                return ref.at[place].at[:, :, columns]
-            return ref.at[:, place].at[:, :, columns]
-
-        def send(axis, origin, step):
-            block = view(slabs, axis, origin)
-            n = index * MESSAGES + count[0]
-            count[0] += 1
-            where = to_z(step) if axis == "z" else to_x(step)
-            copy = remote(block, block, gather_send.at[n], gather_recv.at[n], where)
-            sent.append(copy)
-            return copy
-
-        up = {}
-        odd = index // 2 % 2
-        for axis in order:
-            at, size = (at_z, NZ) if axis == "z" else (at_x, NX)
-            right, left = send(axis, at(0), 1), send(axis, at(0), -1)
-            yield
-            for hop in range(1, size // 2):
-                last = hop == size // 2 - 1
-                right.wait_recv()
-                if not last or not odd:
-                    right_next = send(axis, at(-hop), 1)
-                left.wait_recv()
-                if not last or odd:
-                    left = send(axis, at(hop), -1)
-                if not last or not odd:
-                    right = right_next
-                yield
-            (left if odd else right).wait_recv()
-
-    def reduce_rounds(index, order, first, width, box_far, box_near):
+        for level, edges in enumerate(TREE):
+            if level:
+                wait_for(boxes[index].at[:len(TREE[level - 1])], gather_recv.at[index, level - 1])
+            for offset, parent in edges:
+                slab = slabs.at[whole(minus(parent))].at[:, columns]
+                remote(
+                    slab, slab, gather_send.at[index], gather_recv.at[index, level], device(minus(parent, offset))
+                )
+            yield False
+        wait_for(boxes[index].at[:len(TREE[-1])], gather_recv.at[index, LEVELS - 1])
+
+    def reduce_rounds(index, first, width):
         columns = pl.ds(first, width)
-        count = [0]
-
-        def view(axis, place):
-            if axis == order[0]:
-                return grads.at[(place, x) if axis == "z" else (z, place)].at[:, columns]
-            if axis == "z":
-                return grads.at[place].at[:, :, columns]
-            return grads.at[:, place].at[:, :, columns]
-
-        odd = index // 2 % 2
-        for axis, box in ((order[1], box_far), (order[0], box_near)):
-            at, size = (at_z, NZ) if axis == "z" else (at_x, NX)
-            far = size // 2
-            slot = [0]
-
-            def send(owner, step):
-                n = index * MESSAGES + count[0]
-                count[0] += 1
-                where = to_z(step) if axis == "z" else to_x(step)
-                landing = box.at[slot[0]]
-                slot[0] += 1
-                copy = remote(view(axis, owner), landing, reduce_send.at[n], reduce_recv.at[n], where)
-                sent.append(copy)
-                return copy, landing
-
-            def take(arrived, owner):
-                arrived[0].wait_recv()
-                mine = view(axis, owner)
-                mine[...] = mine[...] + arrived[1][...]
-
-            sign = 1 if odd else -1
-            long = send(at(sign * far), sign)
-            short = send(at(-sign * (far - 1)), -sign)
-            yield
-            for hop in range(1, far):
-                take(long, at(sign * (far - hop)))
-                long = send(at(sign * (far - hop)), sign)
-                if hop < far - 1:
-                    take(short, at(-sign * (far - 1 - hop)))
-                    short = send(at(-sign * (far - 1 - hop)), -sign)
-                yield
-            take(short, at(0))
-            take(long, at(0))
+        box = boxes[index]
+        starts = [sum(len(edges) for edges in TREE[:level]) for level in range(LEVELS)]
+
+        def gathered(offset, level):
+            mine = grads.at[whole(minus(offset))].at[:, columns]
+            total = None
+            for n, (_, parent) in enumerate(TREE[level] if level < LEVELS else ()):
+                if parent == offset:
+                    n += starts[level]
+                    total = box[n] if total is None else total + box[n]
+            if total is not None:
+                mine[...] = mine[...] + total
+            return mine
+
+        def landed(level):
+            if level < LEVELS:
+                wait_for(box.at[pl.ds(starts[level], len(TREE[level]))], reduce_recv.at[index, level])
+
+        for level in reversed(range(LEVELS)):
+            landed(level + 1)
+            for n, (offset, parent) in enumerate(TREE[level]):
+                remote(
+                    gathered(offset, level + 1), box.at[starts[level] + n], reduce_send.at[index],
+                    reduce_recv.at[index, level], device(minus(offset, parent)),
+                )
+            yield False
+        landed(0)
+        gathered((0, 0), 0)
 
     cad_copy.wait()
     cad_in = [
@@ -181,17 +194,26 @@
     ]
     sent.extend(cad_in)
     gathers = [gather_rounds(i, *chunk) for i, chunk in enumerate(CHUNKS)]
-    for g in gathers:
-        next(g)
+    reduces = [reduce_rounds(i, *chunk) for i, chunk in enumerate(CHUNKS)]
+    begun = []
+
+    def advance(rounds):
+        for g in tuple(rounds):
+            if next(g, True):
+                rounds.remove(g)
+
+    advance(list(gathers))
     light_copy.start()
-    for g in gathers:
-        next(g)
+    ahead, others = gathers[:1], gathers[1:]
+    advance(list(ahead))
+    advance(list(others))
+    advance(list(ahead))
     for copy in cad_in:
         copy.wait_recv()
     cad_across = remote(cads.at[:, core], cads.at[:, core], small_send.at[7], small_recv.at[7], partner)
     sent.append(cad_across)
-    for g in gathers:
-        next(g)
+    advance(list(others))
+    advance(list(ahead))
     cad_across.wait_recv()
 
     good_copy.wait()
@@ -210,15 +232,9 @@
     acc[...] = jnp.zeros_like(acc)
     logs[...] = jnp.zeros_like(logs)
 
-    going = True
-    while going:
-        going = False
-        for g in gathers:
-            try:
-                next(g)
-                going = True
-            except StopIteration:
-                pass
+    for _ in range(3, LEVELS):
+        advance(list(others))
+        advance(list(ahead))
     light_copy.wait()
 
     def block(j, carry):
@@ -242,11 +258,11 @@
         acc[...] += dot3(split(loads), weighted, ((1,), (0,))).reshape(acc.shape)
         return carry
 
-    lax.fori_loop(0, HALF // BLOCK, block, 0)
-
-    reduces = [reduce_rounds(i, *chunk, boxes[2 * i], boxes[2 * i + 1]) for i, chunk in enumerate(CHUNKS)]
-    for g in reduces:
-        next(g)
+    for i, (first, width) in enumerate(CHUNKS):
+        next(gathers[i], None)
+        lax.fori_loop(first // BLOCK, (first + width) // BLOCK, block, 0)
+        begun.append(reduces[i])
+        advance(begun)
 
     top = lax.broadcasted_iota(jnp.int32, (16, 8, CADS), 1) < 4
     first, second = acc[:, 0, :, :], acc[:, 1, :, :]
@@ -260,8 +276,6 @@
     cad_part[:, :, 8:16, :] = jnp.broadcast_to(log_sum[None, None], (NY, 2, 8, CADS))
     across = remote(cad_part.at[:, 1 - core], cad_core, small_send.at[8], small_recv.at[8], partner)
     sent.append(across)
-    for g in reduces:
-        next(g)
     across.wait_recv()
     cad_part[:, core] = cad_part[:, core] + cad_core[...]
     arrivals = [
@@ -269,21 +283,22 @@
         for d in range(1, NY)
     ]
     sent.extend(arrivals)
-    for g in reduces:
-        next(g)
     cad_from[y] = cad_part[y, core]
+    advance(begun)
+    for i in range(len(CHUNKS)):
+        wait_for(boxes[i], gather_send.at[i])
+    advance(begun)
     for copy in arrivals:
         copy.wait_recv()
     total = jnp.sum(cad_from[...], axis=0)
-    cad_out[...] = total[0:8] * cad_scale
     loss_x[x] = total[8:16]
     loss_hops = [
         remote(loss_x.at[x], loss_x.at[x], small_send.at[15 + d], small_recv.at[15 + d], to_x(d))
         for d in range(1, NX)
     ]
     sent.extend(loss_hops)
-    for g in reduces:
-        next(g)
+    cad_out[...] = total[0:8] * cad_scale
+    advance(begun)
     for copy in loss_hops:
         copy.wait_recv()
     loss_z[z] = jnp.sum(loss_x[...], axis=0)
@@ -291,44 +306,31 @@
         remote(loss_z.at[z], loss_z.at[z], small_send.at[18 + d], small_recv.at[18 + d], to_z(d))
         for d in range(1, NZ)
     ]
-    sent.extend(loss_hops)
-    for g in reduces:
-        next(g)
-    going = True
-    while going:
-        going = False
-        for g in reduces:
-            try:
-                next(g)
-                going = True
-            except StopIteration:
-                pass
+    advance(begun)
+    for copy in sent:
+        copy.wait_send()
+    advance(begun)
     for copy in loss_hops:
         copy.wait_recv()
     everything = jnp.sum(loss_z[...], axis=0)
     loss_out[...] = jnp.sum(jnp.sum(everything, axis=0, keepdims=True), axis=1, keepdims=True) * loss_scale
-    star_out[:, :HALF] = slabs_out(grads, z, x, 0) * star_scale
-    star_out[:, HALF:] = slabs_out(grads, z, x, 4) * star_scale
-    for copy in sent:
+    for copy in loss_hops:
         copy.wait_send()
-
-
-def slabs_out(grads, z, x, row):
-    return grads[z, x, row:row + 4, :]
+    while begun:
+        advance(begun)
+    for i in range(len(CHUNKS)):
+        wait_for(boxes[i], reduce_send.at[i])
+    star_out[:, :HALF] = grads[z, x, 0:4, :] * star_scale
+    star_out[:, HALF:] = grads[z, x, 4:8, :] * star_scale
 
 
 def on_device(light, quality, star_factors, cadence_factors):
     stars = light.shape[0] * lax.axis_size("star")
     cads = light.shape[1] * lax.axis_size("cad")
     dma = pltpu.SemaphoreType.DMA
-    boxes = []
-    for order, _, width in CHUNKS:
-        far, near = ((NX, NZ) if order == "xz" else (NZ, NX))
-        hops = {NX: 3, NZ: 7}
-        boxes.append(pltpu.VMEM((hops[near], far, 8, width), F32))
-        boxes.append(pltpu.VMEM((hops[far], 8, width), F32))
-    count = len(CHUNKS) * MESSAGES
-    any_space = pl.BlockSpec(memory_space=pl.ANY)
+    boxes = [pltpu.VMEM((EDGES, 8, width), F32) for _, width in CHUNKS]
+    count = len(CHUNKS)
+    hbm = pl.BlockSpec(memory_space=pltpu.HBM)
     vmem = pl.BlockSpec(memory_space=pltpu.VMEM)
     star_gradient, cadence_gradient, loss = pl.pallas_call(
         functools.partial(
@@ -339,7 +341,7 @@
             jax.ShapeDtypeStruct((8, CADS), F32),
             jax.ShapeDtypeStruct((1, 1), F32),
         ),
-        in_specs=[any_space] * 4,
+        in_specs=[hbm] * 4,
         out_specs=(vmem, vmem, vmem),
         scratch_shapes=[
             pltpu.VMEM((4096, CADS), F32),
@@ -360,14 +362,17 @@
             pltpu.VMEM((NZ, 8, CADS), F32),
             *boxes,
             dma((4,)),
-            dma((count,)), dma((count,)), dma((count,)), dma((count,)), dma((26,)), dma((26,)),
+            dma((count,)), dma((count, LEVELS)), dma((count,)), dma((count, LEVELS)), dma((26,)), dma((26,)),
         ],
         compiler_params=pltpu.CompilerParams(
-            collective_id=0, has_side_effects=True, vmem_limit_bytes=60 << 20
+            collective_id=0, has_side_effects=True, vmem_limit_bytes=40 << 20
         ),
         cost_estimate=pl.CostEstimate(flops=10**9, bytes_accessed=5 * 10**6, transcendentals=2 * 10**6),
         name="cauchy_factor_gradient",
-    )(light, quality.reshape(1, CADS), star_factors.T, cadence_factors.T)
+    )(*(
+        pltpu.with_memory_space_constraint(array, pltpu.HBM)
+        for array in (light, quality.reshape(1, CADS), star_factors.T, cadence_factors.T)
+    ))
     return (star_gradient.T, cadence_gradient.T, loss.reshape(()))
 
 

time: 79.6 us -> 67.3 us (0.85)
  Pallas kernels: 74.3 us -> 63.5 us
  local copies, waits for them, and re-layouts: 2.77 us -> 1.23 us
    pallas_call x1, Pallas kernels: 74.3 us -> 63.5 us  [on_device(): pl.pallas_call(functools.partial(kernel, -1.0 / float(cads) ** 0.5, -1.0...]
    unnamed x2, local copies, waits for them, and re-layouts: 2.77 us -> 1.23 us
where the time goes in v2:
time: 67.3 us; the launch traced here: 67.1 us
  Pallas kernels  63.5 us (94%)
  between operations  2.33 us (3%)
  local copies, waits for them, and re-layouts  1.23 us (2%)
    pallas_call x1, Pallas kernels, on_device(): pl.pallas_call(functools.partial(kernel, -1.0 / float(cads) ** 0.5, -1.0...  63.5 us

profile of v2, /device:TPU:2, one launch (start us, length us, event | category | flops | bytes accessed | tf_op | source)
XLA Modules:
  0.0 67.1 jit_solution(7521940876973500877)
XLA Ops:
  0.6 63.5 %cauchy_factor_gradient.1 = (f32[4,4096]{1,0:T(4,128)S(1)}, f32[8,256]{1,0:T(8,128)S(1)}, f32[1,1]{1,0:T(1,128)}) custom-call(f32[4096,256]{1,0:T(8,128)} %light_ref.1, s32[1,256]{1,0:T(1,128)} %bitcast.10, f32[4,4096]{1,0:T(4,128)} %bitcast.8, f32[8,256]{1,0:T(8,128)} %bitcast.9), custom_call_target="tpu_custom_call" | custom-call | flops 1000000000 | bytes 5000000 | tf_op jit(solution)/shard_map/cauchy_factor_gradient/pallas_call | solution.py:335
  64.2 0.6 copy.10
  64.8 0.6 copy.11

commit v3 on v2

--- a/solution.py
+++ b/solution.py
@@ -55,7 +55,7 @@
 
 TREE = tree()
 LEVELS = len(TREE)
-CHUNKS = ((0, 256), (256, 768), (1024, 512), (1536, 512))
+CHUNKS = ((0, 512), (512, 512), (1024, 512), (1536, 512))
 
 
 def split(value):
@@ -67,7 +67,9 @@
     def one(p, q):
         return lax.dot_general(p, q, (dims, ((), ())), preferred_element_type=F32)
 
-    return one(a[0], b[0]) + (one(a[0], b[1]) + one(a[1], b[0]))
+    rows = a[0].shape[0]
+    both = one(jnp.concatenate(a, axis=0), b[0])
+    return both[:rows] + (one(a[0], b[1]) + both[rows:])
 
 
 def kernel(
@@ -75,7 +77,7 @@
     light_ref, quality_ref, star_ref, cad_ref,
     star_out, cad_out, loss_out,
     light, own, slabs, grads, cads, expanded, wide_high, wide_low, good, acc, logs,
-    cad_part, cad_core, cad_from, loss_x, loss_z, *rest,
+    cad_part, cad_core, cad_from, loss_core, loss_y, loss_x, loss_z, *rest,
 ):
     boxes, (sems, gather_send, gather_recv, reduce_send, reduce_recv, small_send, small_recv) = rest[:-7], rest[-7:]
     star, cad = lax.axis_index("star"), lax.axis_index("cad")
@@ -195,7 +197,6 @@
     sent.extend(cad_in)
     gathers = [gather_rounds(i, *chunk) for i, chunk in enumerate(CHUNKS)]
     reduces = [reduce_rounds(i, *chunk) for i, chunk in enumerate(CHUNKS)]
-    begun = []
 
     def advance(rounds):
         for g in tuple(rounds):
@@ -249,7 +250,7 @@
             side = slice(half * CADS, (half + 1) * CADS)
             residual = light[rows, :] * keep - predicted[:, side]
             ratio = 1.0 + (residual * 0.5) ** 2
-            weighted.append(residual / ratio)
+            weighted.append(residual * pl.reciprocal(ratio))
             four = ratio.reshape(4, BLOCK // 4, CADS)
             four = (four[0] * four[1]) * (four[2] * four[3])
             logs[:, side] += jnp.sum(jnp.log(four).reshape(BLOCK // 32, 8, CADS), axis=0)
@@ -258,11 +259,19 @@
         acc[...] += dot3(split(loads), weighted, ((1,), (0,))).reshape(acc.shape)
         return carry
 
+    def step(*which):
+        for i in which:
+            next(reduces[i], None)
+
     for i, (first, width) in enumerate(CHUNKS):
         next(gathers[i], None)
-        lax.fori_loop(first // BLOCK, (first + width) // BLOCK, block, 0)
-        begun.append(reduces[i])
-        advance(begun)
+        lax.fori_loop(first // BLOCK, (first + width) // BLOCK, block, 0, unroll=True)
+        step(*range(i, -1, -2))
+
+    log_sum = (logs[:, :128] + logs[:, 128:256]) + (logs[:, 256:384] + logs[:, 384:])
+    loss_core[core] = log_sum
+    loss_hop = remote(loss_core.at[core], loss_core.at[core], small_send.at[25], small_recv.at[25], partner)
+    sent.append(loss_hop)
 
     top = lax.broadcasted_iota(jnp.int32, (16, 8, CADS), 1) < 4
     first, second = acc[:, 0, :, :], acc[:, 1, :, :]
@@ -271,53 +280,55 @@
         first[:, :, :CADS] + pltpu.roll(first[:, :, CADS:], 4, 1),
         pltpu.roll(second[:, :, :CADS], 4, 1) + second[:, :, CADS:],
     )
-    cad_part[:, :, 0:8, :] = sums.reshape(NY, 2, 8, CADS)
-    log_sum = (logs[:, :CADS] + logs[:, CADS:])
-    cad_part[:, :, 8:16, :] = jnp.broadcast_to(log_sum[None, None], (NY, 2, 8, CADS))
+    cad_part[...] = sums.reshape(NY, 2, 8, CADS)
     across = remote(cad_part.at[:, 1 - core], cad_core, small_send.at[8], small_recv.at[8], partner)
     sent.append(across)
+
+    def exchange(ref, place, first, peers):
+        copies = [
+            remote(ref.at[place], ref.at[place], small_send.at[first + n], small_recv.at[first + n], peer)
+            for n, peer in enumerate(peers)
+        ]
+        sent.extend(copies)
+        return copies
+
+    def arrive(copies):
+        for copy in copies:
+            copy.wait_recv()
+
+    last = len(CHUNKS) - 1
+    older = tuple(range(last - 1, -1, -1))
+    loss_hop.wait_recv()
+    loss_y[y] = loss_core[0] + loss_core[1]
+    loss_hops = exchange(loss_y, y, 26, [to_y(d) for d in range(1, NY)])
     across.wait_recv()
     cad_part[:, core] = cad_part[:, core] + cad_core[...]
+    cad_from[y] = cad_part[y, core]
     arrivals = [
         remote(cad_part.at[at_y(d), core], cad_from.at[y], small_send.at[8 + d], small_recv.at[8 + d], to_y(d))
         for d in range(1, NY)
     ]
     sent.extend(arrivals)
-    cad_from[y] = cad_part[y, core]
-    advance(begun)
+    step(last - 1, last, *older)
+    arrive(loss_hops)
+    loss_x[x] = jnp.sum(loss_y[...], axis=0)
+    loss_hops = exchange(loss_x, x, 16, [to_x(d) for d in range(1, NX)])
+    step(last, *older)
+    arrive(loss_hops)
+    loss_z[z] = jnp.sum(loss_x[...], axis=0)
+    loss_hops = exchange(loss_z, z, 19, [to_z(d) for d in range(1, NZ - 1)]) + exchange(loss_z, z, 33, [to_z(NZ - 1)])
+    step(last, *older)
+    arrive(arrivals)
+    cad_out[...] = jnp.sum(cad_from[...], axis=0) * cad_scale
     for i in range(len(CHUNKS)):
         wait_for(boxes[i], gather_send.at[i])
-    advance(begun)
-    for copy in arrivals:
-        copy.wait_recv()
-    total = jnp.sum(cad_from[...], axis=0)
-    loss_x[x] = total[8:16]
-    loss_hops = [
-        remote(loss_x.at[x], loss_x.at[x], small_send.at[15 + d], small_recv.at[15 + d], to_x(d))
-        for d in range(1, NX)
-    ]
-    sent.extend(loss_hops)
-    cad_out[...] = total[0:8] * cad_scale
-    advance(begun)
-    for copy in loss_hops:
-        copy.wait_recv()
-    loss_z[z] = jnp.sum(loss_x[...], axis=0)
-    loss_hops = [
-        remote(loss_z.at[z], loss_z.at[z], small_send.at[18 + d], small_recv.at[18 + d], to_z(d))
-        for d in range(1, NZ)
-    ]
-    advance(begun)
     for copy in sent:
         copy.wait_send()
-    advance(begun)
-    for copy in loss_hops:
-        copy.wait_recv()
+    arrive(loss_hops)
     everything = jnp.sum(loss_z[...], axis=0)
     loss_out[...] = jnp.sum(jnp.sum(everything, axis=0, keepdims=True), axis=1, keepdims=True) * loss_scale
-    for copy in loss_hops:
-        copy.wait_send()
-    while begun:
-        advance(begun)
+    for _ in range(LEVELS):
+        step(*range(len(CHUNKS)))
     for i in range(len(CHUNKS)):
         wait_for(boxes[i], reduce_send.at[i])
     star_out[:, :HALF] = grads[z, x, 0:4, :] * star_scale
@@ -355,14 +366,16 @@
             pltpu.VMEM((1, CADS), jnp.int32),
             pltpu.VMEM((16, 2, 8, 2 * CADS), F32),
             pltpu.VMEM((8, 2 * CADS), F32),
-            pltpu.VMEM((NY, 2, 16, CADS), F32),
-            pltpu.VMEM((NY, 16, CADS), F32),
-            pltpu.VMEM((NY, 16, CADS), F32),
-            pltpu.VMEM((NX, 8, CADS), F32),
-            pltpu.VMEM((NZ, 8, CADS), F32),
+            pltpu.VMEM((NY, 2, 8, CADS), F32),
+            pltpu.VMEM((NY, 8, CADS), F32),
+            pltpu.VMEM((NY, 8, CADS), F32),
+            pltpu.VMEM((2, 8, 128), F32),
+            pltpu.VMEM((NY, 8, 128), F32),
+            pltpu.VMEM((NX, 8, 128), F32),
+            pltpu.VMEM((NZ, 8, 128), F32),
             *boxes,
             dma((4,)),
-            dma((count,)), dma((count, LEVELS)), dma((count,)), dma((count, LEVELS)), dma((26,)), dma((26,)),
+            dma((count,)), dma((count, LEVELS)), dma((count,)), dma((count, LEVELS)), dma((34,)), dma((34,)),
         ],
         compiler_params=pltpu.CompilerParams(
             collective_id=0, has_side_effects=True, vmem_limit_bytes=40 << 20

time: 67.3 us -> 59.3 us (0.88)
  the two profiles are of different devices: /device:TPU:2 before, /device:TPU:8 now
where the time goes in v3:
time: 59.3 us; the launch traced here: 59.1 us
  Pallas kernels  55.5 us (94%)
  between operations  2.33 us (4%)
  local copies, waits for them, and re-layouts  1.23 us (2%)
    pallas_call x1, Pallas kernels, on_device(): pl.pallas_call(functools.partial(kernel, -1.0 / float(cads) ** 0.5, -1.0...  55.5 us
    unnamed x2, local copies, waits for them, and re-layouts  1.23 us

profile of v3, /device:TPU:8, one launch (start us, length us, event | category | flops | bytes accessed | tf_op | source)
XLA Modules:
  0.0 59.1 jit_solution(15006303938023403437)
XLA Ops:
  0.6 55.5 %cauchy_factor_gradient.1 = (f32[4,4096]{1,0:T(4,128)S(1)}, f32[8,256]{1,0:T(8,128)S(1)}, f32[1,1]{1,0:T(1,128)}) custom-call(f32[4096,256]{1,0:T(8,128)} %light_ref.1, s32[1,256]{1,0:T(1,128)} %bitcast.10, f32[4,4096]{1,0:T(4,128)} %bitcast.8, f32[8,256]{1,0:T(8,128)} %bitcast.9), custom_call_target="tpu_custom_call" | custom-call | flops 1000000000 | bytes 5000000 | tf_op jit(solution)/shard_map/cauchy_factor_gradient/pallas_call | solution.py:346
  56.2 0.6 %copy.10 = f32[4096,4]{0,1:T(4,128)} copy(f32[4096,4]{0,1:T(4,128)S(1)} %bitcast.6) | data formatting | bytes 131072
  56.8 0.6 %copy.11 = f32[256,8]{0,1:T(8,128)} copy(f32[256,8]{0,1:T(8,128)S(1)} %bitcast.7) | data formatting | bytes 16384

commit v4 on v3

--- a/solution.py
+++ b/solution.py
@@ -56,6 +56,8 @@
 TREE = tree()
 LEVELS = len(TREE)
 CHUNKS = ((0, 512), (512, 512), (1024, 512), (1536, 512))
+AFTER = ((), (0,), (), (1,), (), (2, 0), (), (3, 1))
+TAIL = ((0, 2), (3, 1, 2, 0), (3, 2, 1, 0), (3, 2, 1, 0))
 
 
 def split(value):
@@ -238,15 +240,15 @@
         advance(list(ahead))
     light_copy.wait()
 
-    def block(j, carry):
-        columns = pl.ds(pl.multiple_of(j * BLOCK, BLOCK), BLOCK)
+    def block(j):
+        columns = pl.ds(j * BLOCK, BLOCK)
         loads = slabs[:, :, :, columns].reshape(256, BLOCK)
         wide = (wide_high[...], wide_low[...])
         predicted = dot3(split(loads.T), wide, ((1,), (0,)))
         keep = good[...].astype(F32)
         weighted = []
         for half in range(2):
-            rows = pl.ds(pl.multiple_of(half * HALF + j * BLOCK, BLOCK), BLOCK)
+            rows = pl.ds(half * HALF + j * BLOCK, BLOCK)
             side = slice(half * CADS, (half + 1) * CADS)
             residual = light[rows, :] * keep - predicted[:, side]
             ratio = 1.0 + (residual * 0.5) ** 2
@@ -257,7 +259,6 @@
         weighted = split(jnp.concatenate(weighted, axis=1))
         grads[:, :, :, columns] = dot3(wide, weighted, ((1,), (1,))).reshape(NZ, NX, 8, BLOCK)
         acc[...] += dot3(split(loads), weighted, ((1,), (0,))).reshape(acc.shape)
-        return carry
 
     def step(*which):
         for i in which:
@@ -265,8 +266,9 @@
 
     for i, (first, width) in enumerate(CHUNKS):
         next(gathers[i], None)
-        lax.fori_loop(first // BLOCK, (first + width) // BLOCK, block, 0, unroll=True)
-        step(*range(i, -1, -2))
+        for j in range(first // BLOCK, (first + width) // BLOCK):
+            block(j)
+            step(*AFTER[j])
 
     log_sum = (logs[:, :128] + logs[:, 128:256]) + (logs[:, 256:384] + logs[:, 384:])
     loss_core[core] = log_sum
@@ -296,8 +298,7 @@
         for copy in copies:
             copy.wait_recv()
 
-    last = len(CHUNKS) - 1
-    older = tuple(range(last - 1, -1, -1))
+    step(*TAIL[0])
     loss_hop.wait_recv()
     loss_y[y] = loss_core[0] + loss_core[1]
     loss_hops = exchange(loss_y, y, 26, [to_y(d) for d in range(1, NY)])
@@ -309,15 +310,15 @@
         for d in range(1, NY)
     ]
     sent.extend(arrivals)
-    step(last - 1, last, *older)
+    step(*TAIL[1])
     arrive(loss_hops)
     loss_x[x] = jnp.sum(loss_y[...], axis=0)
     loss_hops = exchange(loss_x, x, 16, [to_x(d) for d in range(1, NX)])
-    step(last, *older)
+    step(*TAIL[2])
     arrive(loss_hops)
     loss_z[z] = jnp.sum(loss_x[...], axis=0)
     loss_hops = exchange(loss_z, z, 19, [to_z(d) for d in range(1, NZ - 1)]) + exchange(loss_z, z, 33, [to_z(NZ - 1)])
-    step(last, *older)
+    step(*TAIL[3])
     arrive(arrivals)
     cad_out[...] = jnp.sum(cad_from[...], axis=0) * cad_scale
     for i in range(len(CHUNKS)):

time: 59.3 us -> 58.9 us (level)
  the two profiles are of different devices: /device:TPU:8 before, /device:TPU:64 now
where the time goes in v4:
time: 58.9 us; the launch traced here: 58.7 us
  Pallas kernels  55.1 us (94%)
  between operations  2.33 us (4%)
  local copies, waits for them, and re-layouts  1.23 us (2%)
    pallas_call x1, Pallas kernels, on_device(): pl.pallas_call(functools.partial(kernel, -1.0 / float(cads) ** 0.5, -1.0...  55.1 us
    unnamed x2, local copies, waits for them, and re-layouts  1.23 us

profile of v4, /device:TPU:64, one launch (start us, length us, event | category | flops | bytes accessed | tf_op | source)
XLA Modules:
  0.0 58.7 jit_solution(15635099521985845151)
XLA Ops:
  0.6 55.1 %cauchy_factor_gradient.1 = (f32[4,4096]{1,0:T(4,128)S(1)}, f32[8,256]{1,0:T(8,128)S(1)}, f32[1,1]{1,0:T(1,128)}) custom-call(f32[4096,256]{1,0:T(8,128)} %light_ref.1, s32[1,256]{1,0:T(1,128)} %bitcast.10, f32[4,4096]{1,0:T(4,128)} %bitcast.8, f32[8,256]{1,0:T(8,128)} %bitcast.9), custom_call_target="tpu_custom_call" | custom-call | flops 1000000000 | bytes 5000000 | tf_op jit(solution)/shard_map/cauchy_factor_gradient/pallas_call | solution.py:347
  55.8 0.6 %copy.10 = f32[4096,4]{0,1:T(4,128)} copy(f32[4096,4]{0,1:T(4,128)S(1)} %bitcast.6) | data formatting | bytes 131072
  56.4 0.6 %copy.11 = f32[256,8]{0,1:T(8,128)} copy(f32[256,8]{0,1:T(8,128)S(1)} %bitcast.7) | data formatting | bytes 16384

commit v5 on v4

--- a/solution.py
+++ b/solution.py
@@ -16,23 +16,23 @@
 EDGES = NZ * NX - 1
 STEP_Z = (
     (0, 0, 0, 0),
-    (1, 0, 0, 0),
-    (1, 1, 1, 0),
+    (1, 1, 0, 1),
     (2, 0, 0, 0),
-    (1, 1, -2, 0),
-    (-1, -1, 0, 0),
-    (-1, -2, 0, 0),
-    (-1, 0, -1, 0),
+    (1, 1, 0, 1),
+    (-1, -1, 1, 1),
+    (-1, -1, 0, -1),
+    (-2, 0, 0, 0),
+    (-1, 0, -1, -1),
 )
 STEP_X = (
-    (0, 1, -1, -1),
+    (0, 1, -2, -1),
+    (0, 0, -1, 0),
     (0, 1, 1, -1),
-    (0, 0, 0, -1),
+    (0, 0, -1, -1),
+    (0, 0, -1, 0),
+    (0, 1, 1, 0),
     (0, 1, 1, -1),
-    (0, 0, 0, -1),
-    (0, 0, 1, -1),
-    (0, 0, 1, -1),
-    (0, 1, 0, -1),
+    (0, 1, 0, 0),
 )
 
 
@@ -117,6 +117,9 @@
     barrier = pltpu.get_barrier_semaphore()
     peers = [to_z(d) for d in range(1, NZ)] + [to_x(d) for d in range(1, NX)]
     peers += [to_y(d) for d in range(1, NY)] + [partner]
+    slants = {(a, b) for row in zip(STEP_Z, STEP_X) for a, b in zip(*row) if a and b}
+    slants |= {(-a, -b) for a, b in slants}
+    peers += [(star, at_z(a) * NX + at_x(b)) for a, b in sorted(slants)]
     for peer in peers:
         pl.semaphore_signal(barrier, inc=1, device_id=peer, device_id_type=MESH)
     own_copy.wait()

time: 58.9 us -> 60 us (1.019)
  the two profiles are of different devices: /device:TPU:64 before, /device:TPU:2 now
where the time goes in v5:
time: 60 us; the launch traced here: 59.9 us
  Pallas kernels  56.3 us (94%)
  between operations  2.33 us (4%)
  local copies, waits for them, and re-layouts  1.23 us (2%)
    pallas_call x1, Pallas kernels, on_device(): pl.pallas_call(functools.partial(kernel, -1.0 / float(cads) ** 0.5, -1.0...  56.3 us
    unnamed x2, local copies, waits for them, and re-layouts  1.23 us

profile of v5, /device:TPU:2, one launch (start us, length us, event | category | flops | bytes accessed | tf_op | source)
XLA Modules:
  0.0 59.9 jit_solution(2757247194552895450)
XLA Ops:
  0.6 56.3 %cauchy_factor_gradient.1 = (f32[4,4096]{1,0:T(4,128)S(1)}, f32[8,256]{1,0:T(8,128)S(1)}, f32[1,1]{1,0:T(1,128)}) custom-call(f32[4096,256]{1,0:T(8,128)} %light_ref.1, s32[1,256]{1,0:T(1,128)} %bitcast.10, f32[4,4096]{1,0:T(4,128)} %bitcast.8, f32[8,256]{1,0:T(8,128)} %bitcast.9), custom_call_target="tpu_custom_call" | custom-call | flops 1000000000 | bytes 5000000 | tf_op jit(solution)/shard_map/cauchy_factor_gradient/pallas_call | solution.py:350
  56.9 0.6 %copy.10 = f32[4096,4]{0,1:T(4,128)} copy(f32[4096,4]{0,1:T(4,128)S(1)} %bitcast.6) | data formatting | bytes 131072
  57.6 0.6 copy.11

commit v6 on v5

--- a/solution.py
+++ b/solution.py
@@ -36,9 +36,31 @@
 )
 
 
-def tree():
+SPREAD_Z = (
+    (0, 0, 0, 0),
+    (1, 0, 0, 0),
+    (1, 1, 1, 0),
+    (2, 0, 0, 0),
+    (1, 1, -2, 0),
+    (-1, -1, 0, 0),
+    (-1, -2, 0, 0),
+    (-1, 0, -1, 0),
+)
+SPREAD_X = (
+    (0, 1, -1, -1),
+    (0, 1, 1, -1),
+    (0, 0, 0, -1),
+    (0, 1, 1, -1),
+    (0, 0, 0, -1),
+    (0, 0, 1, -1),
+    (0, 0, 1, -1),
+    (0, 1, 0, -1),
+)
+
+
+def tree(step_z, step_x):
     parents = {
-        (dz, dx): ((dz - STEP_Z[dz][dx]) % NZ, (dx - STEP_X[dz][dx]) % NX)
+        (dz, dx): ((dz - step_z[dz][dx]) % NZ, (dx - step_x[dz][dx]) % NX)
         for dz in range(NZ)
         for dx in range(NX)
         if dz or dx
@@ -53,7 +75,7 @@
     return levels
 
 
-TREE = tree()
+TREE, SPREAD = tree(STEP_Z, STEP_X), tree(SPREAD_Z, SPREAD_X)
 LEVELS = len(TREE)
 CHUNKS = ((0, 512), (512, 512), (1024, 512), (1536, 512))
 AFTER = ((), (0,), (), (1,), (), (2, 0), (), (3, 1))
@@ -152,16 +174,16 @@
 
     def gather_rounds(index, first, width):
         columns = pl.ds(first, width)
-        for level, edges in enumerate(TREE):
+        for level, edges in enumerate(SPREAD):
             if level:
-                wait_for(boxes[index].at[:len(TREE[level - 1])], gather_recv.at[index, level - 1])
+                wait_for(boxes[index].at[:len(SPREAD[level - 1])], gather_recv.at[index, level - 1])
             for offset, parent in edges:
                 slab = slabs.at[whole(minus(parent))].at[:, columns]
                 remote(
                     slab, slab, gather_send.at[index], gather_recv.at[index, level], device(minus(parent, offset))
                 )
             yield False
-        wait_for(boxes[index].at[:len(TREE[-1])], gather_recv.at[index, LEVELS - 1])
+        wait_for(boxes[index].at[:len(SPREAD[-1])], gather_recv.at[index, len(SPREAD) - 1])
 
     def reduce_rounds(index, first, width):
         columns = pl.ds(first, width)
@@ -238,7 +260,7 @@
     acc[...] = jnp.zeros_like(acc)
     logs[...] = jnp.zeros_like(logs)
 
-    for _ in range(3, LEVELS):
+    for _ in range(3, len(SPREAD)):
         advance(list(others))
         advance(list(ahead))
     light_copy.wait()
@@ -379,7 +401,7 @@
             pltpu.VMEM((NZ, 8, 128), F32),
             *boxes,
             dma((4,)),
-            dma((count,)), dma((count, LEVELS)), dma((count,)), dma((count, LEVELS)), dma((34,)), dma((34,)),
+            dma((count,)), dma((count, len(SPREAD))), dma((count,)), dma((count, LEVELS)), dma((34,)), dma((34,)),
         ],
         compiler_params=pltpu.CompilerParams(
             collective_id=0, has_side_effects=True, vmem_limit_bytes=40 << 20

time: 60 us -> 60.7 us (1.012)
    pallas_call x1, Pallas kernels: 56.3 us -> 56.9 us  [on_device(): pl.pallas_call(functools.partial(kernel, -1.0 / float(cads) ** 0.5, -1.0...]
where the time goes in v6:
time: 60.7 us; the launch traced here: 60.5 us
  Pallas kernels  56.9 us (94%)
  between operations  2.33 us (4%)
  local copies, waits for them, and re-layouts  1.23 us (2%)
    pallas_call x1, Pallas kernels, on_device(): pl.pallas_call(functools.partial(kernel, -1.0 / float(cads) ** 0.5, -1.0...  56.9 us
    unnamed x2, local copies, waits for them, and re-layouts  1.23 us

profile of v6, /device:TPU:2, one launch (start us, length us, event | category | flops | bytes accessed | tf_op | source)
XLA Modules:
  0.0 60.5 jit_solution(12945014094850616993)
XLA Ops:
  0.6 56.9 %cauchy_factor_gradient.1 = (f32[4,4096]{1,0:T(4,128)S(1)}, f32[8,256]{1,0:T(8,128)S(1)}, f32[1,1]{1,0:T(1,128)}) custom-call(f32[4096,256]{1,0:T(8,128)} %light_ref.1, s32[1,256]{1,0:T(1,128)} %bitcast.10, f32[4,4096]{1,0:T(4,128)} %bitcast.8, f32[8,256]{1,0:T(8,128)} %bitcast.9), custom_call_target="tpu_custom_call" | custom-call | flops 1000000000 | bytes 5000000 | tf_op jit(solution)/shard_map/cauchy_factor_gradient/pallas_call | solution.py:372
  57.6 0.6 %copy.10 = f32[4096,4]{0,1:T(4,128)} copy(f32[4096,4]{0,1:T(4,128)S(1)} %bitcast.6) | data formatting | bytes 131072
  58.2 0.6 copy.11
